TPU v7x, 32 devices: a whole 2x2x4 slice. The times are simulated.
32 devices in a mesh: ray: 4 (over y, core), cuts: 8 (over z, x).
Axes of the slice: x: 2, y: 2, z: 4, core: 2. Of those that a mesh axis runs over, the one named last changes fastest.
Arguments:
- initial: float32 [16, 16, 4096], P('cuts', 'ray'), may hold values from 0.5 to 1.5
- measured: float32 [4, 32, 16, 4096], P('ray', None, 'cuts'), may hold values from 9.6 to 28.8
- order: int32 [4], replicated, may hold values from 0 to 3, each once
- angle_index: int32 [4, 32], replicated, may hold values from 0 to 2999
Outputs:
- reconstruction: float32 [16, 16, 4096], P('cuts', 'ray')
Inputs may be any that keep to these rules, and one draw needn't show every extreme that they name: Each stored subset appears once; the first 2 entries are the subsets run, in order, and stored subset j is held by index j of ray.
All inputs are finite; a program needn't handle non-finite values.
Results may differ from a plain program's by a relative error of at most 0.0003.
Values sent between devices are 32-bit elements; how exact they have to be, the bound alone decides.
No kernel may reach another device: no remote copies, remote signals or barrier semaphores. Data moves between devices by JAX's collectives and lax.ppermute only.
A program may use at most 64 MiB of HBM per device.

v0:
```python
import jax
import jax.numpy as jnp
from jax import lax
from jax.sharding import PartitionSpec as P

SUBSETS = 2
NANG = 3000
TV_ITERS = 2
TV_STEP = 0.05
TV_EPS = 0.5
angle_group = 2


def broadcast(value, axis, source):
    kept = jnp.where(lax.axis_index(axis) == source, value, 0).astype(value.dtype)
    return lax.psum(kept, axis)


def padded_2(block, sides, width):
    for axis, dim in sides:
        count = lax.axis_size(axis)
        forward = [(i, i + 1) for i in range(count - 1)]
        backward = [(target, source) for source, target in forward]
        low = lax.ppermute(
            lax.slice_in_dim(block, block.shape[dim] - width, None, axis=dim), axis, forward
        )
        high = lax.ppermute(lax.slice_in_dim(block, 0, width, axis=dim), axis, backward)
        block = jnp.concatenate([low, block, high], axis=dim)
    return block


def strip_geometry(angle_row, first_row, total_rows, strip_rows):
    slopes = -1.0 + (2.0 * angle_row.astype(jnp.float32) + 1.0) / NANG
    row_pos = (first_row + jnp.arange(strip_rows, dtype=jnp.int32)).astype(jnp.float32) - (
        total_rows - 1
    ) / 2.0
    spread = slopes[:, None] * row_pos[None, :]
    floor_part = jnp.floor(spread)
    return (floor_part.astype(jnp.int32), spread - floor_part)


def row_windows(padded, starts, width):

    def row_one_row(plane, start):
        return lax.dynamic_slice_in_dim(plane, start, width, 1)

    return jax.vmap(row_one_row, in_axes=(1, 0), out_axes=1)(padded, starts)


def plane_windows(plane, starts, width):

    def plane_one_row(start):
        return lax.dynamic_slice_in_dim(plane, start, width, 1)

    return jax.vmap(plane_one_row, out_axes=1)(starts)


def project_block(padded, shifts, fraction, margin, width):
    angle_count, rows = shifts.shape
    groups = angle_count // angle_group

    def project_one_angle(shift_row, frac_row):
        window = row_windows(padded, margin - shift_row - 1, width + 1)
        weight = frac_row[None, :, None]
        return jnp.sum((1.0 - weight) * window[:, :, 1:] + weight * window[:, :, :-1], axis=1)

    def one_group(pieces):
        return jax.vmap(project_one_angle)(pieces[0], pieces[1])

    result = lax.map(
        one_group,
        (shifts.reshape(groups, angle_group, rows), fraction.reshape(groups, angle_group, rows)),
    )
    return result.reshape(angle_count, padded.shape[0], width)


def back_block(res_padded, shifts, fraction, margin, width):
    angle_count, rows = shifts.shape
    groups = angle_count // angle_group
    slices = res_padded.shape[1]

    def back_one_angle(plane, shift_row, frac_row):
        window = plane_windows(plane, margin + shift_row, width + 1)
        weight = frac_row[None, :, None]
        return (1.0 - weight) * window[:, :, :-1] + weight * window[:, :, 1:]

    def add_group(summed, pieces):
        terms = jax.vmap(back_one_angle)(pieces[0], pieces[1], pieces[2])
        return (summed + jnp.sum(terms, axis=0), None)

    planes = res_padded.reshape((groups, angle_group) + res_padded.shape[1:])
    summed, _ = lax.scan(
        add_group,
        jnp.zeros((slices, rows, width), jnp.float32),
        (
            planes,
            shifts.reshape(groups, angle_group, rows),
            fraction.reshape(groups, angle_group, rows),
        ),
    )
    return summed


def tv_step(extended, first_row, first_slice, total_rows, total_slices):
    count_s, count_r, breadth = extended.shape
    row_ids = first_row + jnp.arange(count_r, dtype=jnp.int32)
    slice_ids = first_slice + jnp.arange(count_s, dtype=jnp.int32)
    row_in = (row_ids >= 0) & (row_ids < total_rows)
    slice_in = (slice_ids >= 0) & (slice_ids < total_slices)
    centre = extended[:-1, :-1]
    cell_in = slice_in[:-1, None] & row_in[None, :-1]
    valid_r = cell_in & row_in[None, 1:]
    valid_s = cell_in & slice_in[1:, None]
    step_r = jnp.where(valid_r[:, :, None], extended[:-1, 1:] - centre, 0.0)
    step_s = jnp.where(valid_s[:, :, None], extended[1:, :-1] - centre, 0.0)
    along_c = jnp.concatenate(
        [centre[:, :, 1:] - centre[:, :, :-1], jnp.zeros_like(centre[:, :, :1])], axis=2
    )
    step_c = jnp.where(cell_in[:, :, None], along_c, 0.0)
    magnitude = jnp.sqrt(step_s * step_s + step_r * step_r + step_c * step_c + TV_EPS * TV_EPS)
    flow_r = step_r / magnitude
    flow_s = step_s / magnitude
    flow_c = step_c / magnitude
    inner_c = flow_c[1:, 1:]
    spread = flow_r[1:, 1:] - flow_r[1:, :-1] + flow_s[1:, 1:] - flow_s[:-1, 1:]
    spread = spread + inner_c - jnp.pad(inner_c[:, :, :-1], ((0, 0), (0, 0), (1, 0)))
    return extended[1:-1, 1:-1] + TV_STEP * spread


def on_device(initial, measured, order, angle_index):
    slices, strip_rows, breadth = initial.shape
    ray_count = lax.axis_size("ray")
    cut_count = lax.axis_size("cuts")
    ray_place = lax.axis_index("ray")
    cut_place = lax.axis_index("cuts")
    total_rows = strip_rows * ray_count
    total_slices = slices * cut_count
    angle_total = angle_index.shape[1]
    margin = total_rows // 2 + 2
    stored = measured[0]
    current = initial
    for subset in range(SUBSETS):
        subset_slot = order[subset]
        shifts, fraction = strip_geometry(
            angle_index[subset_slot], ray_place * strip_rows, total_rows, strip_rows
        )
        padded = jnp.pad(current, ((0, 0), (0, 0), (margin, margin)))
        partial_value = project_block(padded, shifts, fraction, margin, breadth)
        totals = lax.psum(partial_value, "ray")
        residual = broadcast(stored - totals, "ray", subset_slot)
        res_padded = jnp.pad(residual, ((0, 0), (0, 0), (margin, margin)))
        current = current + back_block(res_padded, shifts, fraction, margin, breadth) / (
            total_rows * angle_total
        )
        for tv_turn in range(TV_ITERS):
            extended = padded_2(current, (("ray", 1), ("cuts", 0)), 1)
            current = tv_step(
                extended,
                ray_place * strip_rows - 1,
                cut_place * slices - 1,
                total_rows,
                total_slices,
            )
    return current


def solution(mesh):
    return jax.shard_map(
        on_device,
        mesh=mesh,
        in_specs=(P("cuts", "ray", None), P("ray", None, "cuts", None), P(), P()),
        out_specs=P("cuts", "ray", None),
        check_vma=False,
    )
```

profile of v0, /device:TPU:1, one launch (start us, length us, event | category | flops | bytes accessed | tf_op | source)
XLA Modules:
  0.0 1349.5 jit_solution(12900914432349245809)
XLA Ops:
  14.4 270.8 %while.65 = (s32[]{:T(128)}, f32[16,2,2,4096]{3,2,1,0:T(2,128)S(1)}, f32[16,2,4]{2,1,0:T(2,128)S(1)}, f32[2,4,4116]{2,0,1:T(2,128)S(1)}, s32[16,2,4]{2,1,0:T(2,128)S(1)}, /*index=5*/s32[]{:T(128)}, s32[]{:T(128)}, s32[]{:T(128)}) while((s32[]{:T(128)}, f32[16,2,2,4096]{3,2,1,0:T(2,128)S(1)}, f32[16,2,4]{2,1,0:T(2,128)S(1)}, ...), condition=%wide.region_2.3_spmd, body=%wide.region_0.2_spmd.sunk | while | flops 245828 | bytes 789350 | solution.py:70
  14.6 16.3 %while.72 = (s32[]{:T(128)}, f32[4,2,4116]{2,1,0:T(2,128)S(1)}, s32[8,3]{0,1:T(4,128)S(1)}, f32[8,2,4097]{2,1,0:T(2,128)S(1)}, s32[]{:T(128)}) while((s32[]{:T(128)}, f32[4,2,4116]{2,1,0:T(2,128)S(1)}, s32[8,3]{0,1:T(4,128)S(1)}, f32[8,2,4097]{2,1,0:T(2,128)S(1)}, s32[]{:T(128)}) %tuple.259), condition=%wide.while_cond, body=%wide.while_body.sunk | while | flops 2 | bytes 67701 | solution.py:45
  48.4 16.3 %while.72 = (s32[]{:T(128)}, f32[4,2,4116]{2,1,0:T(2,128)S(1)}, s32[8,3]{0,1:T(4,128)S(1)}, f32[8,2,4097]{2,1,0:T(2,128)S(1)}, s32[]{:T(128)}) while((s32[]{:T(128)}, f32[4,2,4116]{2,1,0:T(2,128)S(1)}, s32[8,3]{0,1:T(4,128)S(1)}, f32[8,2,4097]{2,1,0:T(2,128)S(1)}, s32[]{:T(128)}) %tuple.259), condition=%wide.while_cond, body=%wide.while_body.sunk | while | flops 2 | bytes 67701 | solution.py:45
  65.4 16.3 %while.72 = (s32[]{:T(128)}, f32[4,2,4116]{2,1,0:T(2,128)S(1)}, s32[8,3]{0,1:T(4,128)S(1)}, f32[8,2,4097]{2,1,0:T(2,128)S(1)}, s32[]{:T(128)}) while((s32[]{:T(128)}, f32[4,2,4116]{2,1,0:T(2,128)S(1)}, s32[8,3]{0,1:T(4,128)S(1)}, f32[8,2,4097]{2,1,0:T(2,128)S(1)}, s32[]{:T(128)}) %tuple.259), condition=%wide.while_cond, body=%wide.while_body.sunk | while | flops 2 | bytes 67701 | solution.py:45
  99.2 16.3 %while.72 = (s32[]{:T(128)}, f32[4,2,4116]{2,1,0:T(2,128)S(1)}, s32[8,3]{0,1:T(4,128)S(1)}, f32[8,2,4097]{2,1,0:T(2,128)S(1)}, s32[]{:T(128)}) while((s32[]{:T(128)}, f32[4,2,4116]{2,1,0:T(2,128)S(1)}, s32[8,3]{0,1:T(4,128)S(1)}, f32[8,2,4097]{2,1,0:T(2,128)S(1)}, s32[]{:T(128)}) %tuple.259), condition=%wide.while_cond, body=%wide.while_body.sunk | while | flops 2 | bytes 67701 | solution.py:45
  133.1 16.3 %while.72 = (s32[]{:T(128)}, f32[4,2,4116]{2,1,0:T(2,128)S(1)}, s32[8,3]{0,1:T(4,128)S(1)}, f32[8,2,4097]{2,1,0:T(2,128)S(1)}, s32[]{:T(128)}) while((s32[]{:T(128)}, f32[4,2,4116]{2,1,0:T(2,128)S(1)}, s32[8,3]{0,1:T(4,128)S(1)}, f32[8,2,4097]{2,1,0:T(2,128)S(1)}, s32[]{:T(128)}) %tuple.259), condition=%wide.while_cond, body=%wide.while_body.sunk | while | flops 2 | bytes 67701 | solution.py:45
  166.9 16.3 %while.72 = (s32[]{:T(128)}, f32[4,2,4116]{2,1,0:T(2,128)S(1)}, s32[8,3]{0,1:T(4,128)S(1)}, f32[8,2,4097]{2,1,0:T(2,128)S(1)}, s32[]{:T(128)}) while((s32[]{:T(128)}, f32[4,2,4116]{2,1,0:T(2,128)S(1)}, s32[8,3]{0,1:T(4,128)S(1)}, f32[8,2,4097]{2,1,0:T(2,128)S(1)}, s32[]{:T(128)}) %tuple.259), condition=%wide.while_cond, body=%wide.while_body.sunk | while | flops 2 | bytes 67701 | solution.py:45
  183.8 16.3 %while.72 = (s32[]{:T(128)}, f32[4,2,4116]{2,1,0:T(2,128)S(1)}, s32[8,3]{0,1:T(4,128)S(1)}, f32[8,2,4097]{2,1,0:T(2,128)S(1)}, s32[]{:T(128)}) while((s32[]{:T(128)}, f32[4,2,4116]{2,1,0:T(2,128)S(1)}, s32[8,3]{0,1:T(4,128)S(1)}, f32[8,2,4097]{2,1,0:T(2,128)S(1)}, s32[]{:T(128)}) %tuple.259), condition=%wide.while_cond, body=%wide.while_body.sunk | while | flops 2 | bytes 67701 | solution.py:45
  217.7 16.3 %while.72 = (s32[]{:T(128)}, f32[4,2,4116]{2,1,0:T(2,128)S(1)}, s32[8,3]{0,1:T(4,128)S(1)}, f32[8,2,4097]{2,1,0:T(2,128)S(1)}, s32[]{:T(128)}) while((s32[]{:T(128)}, f32[4,2,4116]{2,1,0:T(2,128)S(1)}, s32[8,3]{0,1:T(4,128)S(1)}, f32[8,2,4097]{2,1,0:T(2,128)S(1)}, s32[]{:T(128)}) %tuple.259), condition=%wide.while_cond, body=%wide.while_body.sunk | while | flops 2 | bytes 67701 | solution.py:45
  287.0 37.4 %all-reduce.21.cloned.1.call-done = f32[32,2,4096]{2,1,0:T(2,128)} async-done(((f32[32,2,4096]{2,1,0:T(2,128)}), f32[32,2,4096]{2,1,0:T(2,128)}) %all-reduce.21.cloned.1.call-update) | async-done | bytes 1048592 | tf_op jit(solution)/shard_map/psum | solution.py:149
  327.6 36.7 %all-reduce.23.cloned.1.call-done = f32[32,2,4096]{2,1,0:T(2,128)} async-done(((f32[32,2,4096]{2,1,0:T(2,128)}), f32[32,2,4096]{2,1,0:T(2,128)}) %all-reduce.23.cloned.1.call-update) | async-done | bytes 1048592 | tf_op jit(solution)/shard_map/psum | solution.py:16
  366.7 274.4 %while.69 = (s32[]{:T(128)}, f32[2,4,4096]{2,0,1:T(2,128)S(1)}, f32[16,2,4]{2,1,0:T(2,128)S(1)}, f32[16,2,2,4116]{3,2,1,0:T(2,128)S(1)}, s32[16,2,4]{2,1,0:T(2,128)S(1)}, /*index=5*/s32[]{:T(128)}, s32[]{:T(128)}, s32[]{:T(128)}) while((s32[]{:T(128)}, f32[2,4,4096]{2,0,1:T(2,128)S(1)}, f32[16,2,4]{2,1,0:T(2,128)S(1)}, ...), condition=%wide.region_7.8_spmd.clone, body=%wide.region_5.7_spmd.clone.sunk | while | flops 294981 | bytes 1248752 | solution.py:92
  366.8 16.3 %while.74 = (s32[]{:T(128)}, f32[2,2,4116]{2,1,0:T(2,128)S(1)}, s32[8,3]{0,1:T(4,128)S(1)}, f32[8,2,4097]{2,1,0:T(2,128)S(1)}, s32[]{:T(128)}) while((s32[]{:T(128)}, f32[2,2,4116]{2,1,0:T(2,128)S(1)}, s32[8,3]{0,1:T(4,128)S(1)}, f32[8,2,4097]{2,1,0:T(2,128)S(1)}, s32[]{:T(128)}) %tuple.230), condition=%wide.while_cond.1, body=%wide.while_body.1.sunk | while | flops 2 | bytes 67701 | solution.py:53
  384.0 16.3 %while.74 = (s32[]{:T(128)}, f32[2,2,4116]{2,1,0:T(2,128)S(1)}, s32[8,3]{0,1:T(4,128)S(1)}, f32[8,2,4097]{2,1,0:T(2,128)S(1)}, s32[]{:T(128)}) while((s32[]{:T(128)}, f32[2,2,4116]{2,1,0:T(2,128)S(1)}, s32[8,3]{0,1:T(4,128)S(1)}, f32[8,2,4097]{2,1,0:T(2,128)S(1)}, s32[]{:T(128)}) %tuple.230), condition=%wide.while_cond.1, body=%wide.while_body.1.sunk | while | flops 2 | bytes 67701 | solution.py:53
  401.1 16.3 %while.74 = (s32[]{:T(128)}, f32[2,2,4116]{2,1,0:T(2,128)S(1)}, s32[8,3]{0,1:T(4,128)S(1)}, f32[8,2,4097]{2,1,0:T(2,128)S(1)}, s32[]{:T(128)}) while((s32[]{:T(128)}, f32[2,2,4116]{2,1,0:T(2,128)S(1)}, s32[8,3]{0,1:T(4,128)S(1)}, f32[8,2,4097]{2,1,0:T(2,128)S(1)}, s32[]{:T(128)}) %tuple.230), condition=%wide.while_cond.1, body=%wide.while_body.1.sunk | while | flops 2 | bytes 67701 | solution.py:53
  418.3 16.3 %while.74 = (s32[]{:T(128)}, f32[2,2,4116]{2,1,0:T(2,128)S(1)}, s32[8,3]{0,1:T(4,128)S(1)}, f32[8,2,4097]{2,1,0:T(2,128)S(1)}, s32[]{:T(128)}) while((s32[]{:T(128)}, f32[2,2,4116]{2,1,0:T(2,128)S(1)}, s32[8,3]{0,1:T(4,128)S(1)}, f32[8,2,4097]{2,1,0:T(2,128)S(1)}, s32[]{:T(128)}) %tuple.230), condition=%wide.while_cond.1, body=%wide.while_body.1.sunk | while | flops 2 | bytes 67701 | solution.py:53
  435.4 16.3 %while.74 = (s32[]{:T(128)}, f32[2,2,4116]{2,1,0:T(2,128)S(1)}, s32[8,3]{0,1:T(4,128)S(1)}, f32[8,2,4097]{2,1,0:T(2,128)S(1)}, s32[]{:T(128)}) while((s32[]{:T(128)}, f32[2,2,4116]{2,1,0:T(2,128)S(1)}, s32[8,3]{0,1:T(4,128)S(1)}, f32[8,2,4097]{2,1,0:T(2,128)S(1)}, s32[]{:T(128)}) %tuple.230), condition=%wide.while_cond.1, body=%wide.while_body.1.sunk | while | flops 2 | bytes 67701 | solution.py:53
  452.6 16.3 %while.74 = (s32[]{:T(128)}, f32[2,2,4116]{2,1,0:T(2,128)S(1)}, s32[8,3]{0,1:T(4,128)S(1)}, f32[8,2,4097]{2,1,0:T(2,128)S(1)}, s32[]{:T(128)}) while((s32[]{:T(128)}, f32[2,2,4116]{2,1,0:T(2,128)S(1)}, s32[8,3]{0,1:T(4,128)S(1)}, f32[8,2,4097]{2,1,0:T(2,128)S(1)}, s32[]{:T(128)}) %tuple.230), condition=%wide.while_cond.1, body=%wide.while_body.1.sunk | while | flops 2 | bytes 67701 | solution.py:53
  469.7 16.3 %while.74 = (s32[]{:T(128)}, f32[2,2,4116]{2,1,0:T(2,128)S(1)}, s32[8,3]{0,1:T(4,128)S(1)}, f32[8,2,4097]{2,1,0:T(2,128)S(1)}, s32[]{:T(128)}) while((s32[]{:T(128)}, f32[2,2,4116]{2,1,0:T(2,128)S(1)}, s32[8,3]{0,1:T(4,128)S(1)}, f32[8,2,4097]{2,1,0:T(2,128)S(1)}, s32[]{:T(128)}) %tuple.230), condition=%wide.while_cond.1, body=%wide.while_body.1.sunk | while | flops 2 | bytes 67701 | solution.py:53
  486.9 16.3 %while.74 = (s32[]{:T(128)}, f32[2,2,4116]{2,1,0:T(2,128)S(1)}, s32[8,3]{0,1:T(4,128)S(1)}, f32[8,2,4097]{2,1,0:T(2,128)S(1)}, s32[]{:T(128)}) while((s32[]{:T(128)}, f32[2,2,4116]{2,1,0:T(2,128)S(1)}, s32[8,3]{0,1:T(4,128)S(1)}, f32[8,2,4097]{2,1,0:T(2,128)S(1)}, s32[]{:T(128)}) %tuple.230), condition=%wide.while_cond.1, body=%wide.while_body.1.sunk | while | flops 2 | bytes 67701 | solution.py:53
  504.0 16.3 %while.74 = (s32[]{:T(128)}, f32[2,2,4116]{2,1,0:T(2,128)S(1)}, s32[8,3]{0,1:T(4,128)S(1)}, f32[8,2,4097]{2,1,0:T(2,128)S(1)}, s32[]{:T(128)}) while((s32[]{:T(128)}, f32[2,2,4116]{2,1,0:T(2,128)S(1)}, s32[8,3]{0,1:T(4,128)S(1)}, f32[8,2,4097]{2,1,0:T(2,128)S(1)}, s32[]{:T(128)}) %tuple.230), condition=%wide.while_cond.1, body=%wide.while_body.1.sunk | while | flops 2 | bytes 67701 | solution.py:53
  521.2 16.3 %while.74 = (s32[]{:T(128)}, f32[2,2,4116]{2,1,0:T(2,128)S(1)}, s32[8,3]{0,1:T(4,128)S(1)}, f32[8,2,4097]{2,1,0:T(2,128)S(1)}, s32[]{:T(128)}) while((s32[]{:T(128)}, f32[2,2,4116]{2,1,0:T(2,128)S(1)}, s32[8,3]{0,1:T(4,128)S(1)}, f32[8,2,4097]{2,1,0:T(2,128)S(1)}, s32[]{:T(128)}) %tuple.230), condition=%wide.while_cond.1, body=%wide.while_body.1.sunk | while | flops 2 | bytes 67701 | solution.py:53
  538.3 16.3 %while.74 = (s32[]{:T(128)}, f32[2,2,4116]{2,1,0:T(2,128)S(1)}, s32[8,3]{0,1:T(4,128)S(1)}, f32[8,2,4097]{2,1,0:T(2,128)S(1)}, s32[]{:T(128)}) while((s32[]{:T(128)}, f32[2,2,4116]{2,1,0:T(2,128)S(1)}, s32[8,3]{0,1:T(4,128)S(1)}, f32[8,2,4097]{2,1,0:T(2,128)S(1)}, s32[]{:T(128)}) %tuple.230), condition=%wide.while_cond.1, body=%wide.while_body.1.sunk | while | flops 2 | bytes 67701 | solution.py:53
  555.5 16.3 %while.74 = (s32[]{:T(128)}, f32[2,2,4116]{2,1,0:T(2,128)S(1)}, s32[8,3]{0,1:T(4,128)S(1)}, f32[8,2,4097]{2,1,0:T(2,128)S(1)}, s32[]{:T(128)}) while((s32[]{:T(128)}, f32[2,2,4116]{2,1,0:T(2,128)S(1)}, s32[8,3]{0,1:T(4,128)S(1)}, f32[8,2,4097]{2,1,0:T(2,128)S(1)}, s32[]{:T(128)}) %tuple.230), condition=%wide.while_cond.1, body=%wide.while_body.1.sunk | while | flops 2 | bytes 67701 | solution.py:53
  572.6 16.3 %while.74 = (s32[]{:T(128)}, f32[2,2,4116]{2,1,0:T(2,128)S(1)}, s32[8,3]{0,1:T(4,128)S(1)}, f32[8,2,4097]{2,1,0:T(2,128)S(1)}, s32[]{:T(128)}) while((s32[]{:T(128)}, f32[2,2,4116]{2,1,0:T(2,128)S(1)}, s32[8,3]{0,1:T(4,128)S(1)}, f32[8,2,4097]{2,1,0:T(2,128)S(1)}, s32[]{:T(128)}) %tuple.230), condition=%wide.while_cond.1, body=%wide.while_body.1.sunk | while | flops 2 | bytes 67701 | solution.py:53
  589.8 16.3 %while.74 = (s32[]{:T(128)}, f32[2,2,4116]{2,1,0:T(2,128)S(1)}, s32[8,3]{0,1:T(4,128)S(1)}, f32[8,2,4097]{2,1,0:T(2,128)S(1)}, s32[]{:T(128)}) while((s32[]{:T(128)}, f32[2,2,4116]{2,1,0:T(2,128)S(1)}, s32[8,3]{0,1:T(4,128)S(1)}, f32[8,2,4097]{2,1,0:T(2,128)S(1)}, s32[]{:T(128)}) %tuple.230), condition=%wide.while_cond.1, body=%wide.while_body.1.sunk | while | flops 2 | bytes 67701 | solution.py:53
  606.9 16.3 %while.74 = (s32[]{:T(128)}, f32[2,2,4116]{2,1,0:T(2,128)S(1)}, s32[8,3]{0,1:T(4,128)S(1)}, f32[8,2,4097]{2,1,0:T(2,128)S(1)}, s32[]{:T(128)}) while((s32[]{:T(128)}, f32[2,2,4116]{2,1,0:T(2,128)S(1)}, s32[8,3]{0,1:T(4,128)S(1)}, f32[8,2,4097]{2,1,0:T(2,128)S(1)}, s32[]{:T(128)}) %tuple.230), condition=%wide.while_cond.1, body=%wide.while_body.1.sunk | while | flops 2 | bytes 67701 | solution.py:53
  624.0 16.3 %while.74 = (s32[]{:T(128)}, f32[2,2,4116]{2,1,0:T(2,128)S(1)}, s32[8,3]{0,1:T(4,128)S(1)}, f32[8,2,4097]{2,1,0:T(2,128)S(1)}, s32[]{:T(128)}) while((s32[]{:T(128)}, f32[2,2,4116]{2,1,0:T(2,128)S(1)}, s32[8,3]{0,1:T(4,128)S(1)}, f32[8,2,4097]{2,1,0:T(2,128)S(1)}, s32[]{:T(128)}) %tuple.230), condition=%wide.while_cond.1, body=%wide.while_body.1.sunk | while | flops 2 | bytes 67701 | solution.py:53
  680.0 270.8 %while.67 = (s32[]{:T(128)}, f32[16,2,2,4096]{3,2,1,0:T(2,128)S(1)}, f32[16,2,4]{2,1,0:T(2,128)S(1)}, f32[2,4,4116]{2,0,1:T(2,128)S(1)}, s32[16,2,4]{2,1,0:T(2,128)S(1)}, /*index=5*/s32[]{:T(128)}, s32[]{:T(128)}, s32[]{:T(128)}) while((s32[]{:T(128)}, f32[16,2,2,4096]{3,2,1,0:T(2,128)S(1)}, f32[16,2,4]{2,1,0:T(2,128)S(1)}, ...), condition=%wide.region_10.11_spmd, body=%wide.region_8.10_spmd.sunk | while | flops 245828 | bytes 789350 | solution.py:70
  952.5 35.1 %all-reduce.25.cloned.1.call-done = f32[32,2,4096]{2,1,0:T(2,128)} async-done(((f32[32,2,4096]{2,1,0:T(2,128)}), f32[32,2,4096]{2,1,0:T(2,128)}) %all-reduce.25.cloned.1.call-update) | async-done | bytes 1048592 | tf_op jit(solution)/shard_map/psum | solution.py:149
  990.5 36.9 %all-reduce.27.cloned.1.call-done = f32[32,2,4096]{2,1,0:T(2,128)} async-done(((f32[32,2,4096]{2,1,0:T(2,128)}), f32[32,2,4096]{2,1,0:T(2,128)}) %all-reduce.27.cloned.1.call-update) | async-done | bytes 1048592 | tf_op jit(solution)/shard_map/psum | solution.py:16
  1029.8 274.4 %while.71 = (s32[]{:T(128)}, f32[2,4,4096]{2,0,1:T(2,128)S(1)}, f32[16,2,4]{2,1,0:T(2,128)S(1)}, f32[16,2,2,4116]{3,2,1,0:T(2,128)S(1)}, s32[16,2,4]{2,1,0:T(2,128)S(1)}, /*index=5*/s32[]{:T(128)}, s32[]{:T(128)}, s32[]{:T(128)}) while((s32[]{:T(128)}, f32[2,4,4096]{2,0,1:T(2,128)S(1)}, f32[16,2,4]{2,1,0:T(2,128)S(1)}, ...), condition=%wide.region_15.16_spmd.clone, body=%wide.region_13.15_spmd.clone.sunk | while | flops 294981 | bytes 1248752 | solution.py:92
  1030.0 16.3 %while.75 = (s32[]{:T(128)}, f32[2,2,4116]{2,1,0:T(2,128)S(1)}, s32[8,3]{0,1:T(4,128)S(1)}, f32[8,2,4097]{2,1,0:T(2,128)S(1)}, s32[]{:T(128)}) while((s32[]{:T(128)}, f32[2,2,4116]{2,1,0:T(2,128)S(1)}, s32[8,3]{0,1:T(4,128)S(1)}, f32[8,2,4097]{2,1,0:T(2,128)S(1)}, s32[]{:T(128)}) %tuple.227), condition=%wide.while_cond.3, body=%wide.while_body.3.sunk | while | flops 2 | bytes 67701 | solution.py:53
  1047.1 16.3 %while.75 = (s32[]{:T(128)}, f32[2,2,4116]{2,1,0:T(2,128)S(1)}, s32[8,3]{0,1:T(4,128)S(1)}, f32[8,2,4097]{2,1,0:T(2,128)S(1)}, s32[]{:T(128)}) while((s32[]{:T(128)}, f32[2,2,4116]{2,1,0:T(2,128)S(1)}, s32[8,3]{0,1:T(4,128)S(1)}, f32[8,2,4097]{2,1,0:T(2,128)S(1)}, s32[]{:T(128)}) %tuple.227), condition=%wide.while_cond.3, body=%wide.while_body.3.sunk | while | flops 2 | bytes 67701 | solution.py:53
  1064.3 16.3 %while.75 = (s32[]{:T(128)}, f32[2,2,4116]{2,1,0:T(2,128)S(1)}, s32[8,3]{0,1:T(4,128)S(1)}, f32[8,2,4097]{2,1,0:T(2,128)S(1)}, s32[]{:T(128)}) while((s32[]{:T(128)}, f32[2,2,4116]{2,1,0:T(2,128)S(1)}, s32[8,3]{0,1:T(4,128)S(1)}, f32[8,2,4097]{2,1,0:T(2,128)S(1)}, s32[]{:T(128)}) %tuple.227), condition=%wide.while_cond.3, body=%wide.while_body.3.sunk | while | flops 2 | bytes 67701 | solution.py:53
  1081.4 16.3 %while.75 = (s32[]{:T(128)}, f32[2,2,4116]{2,1,0:T(2,128)S(1)}, s32[8,3]{0,1:T(4,128)S(1)}, f32[8,2,4097]{2,1,0:T(2,128)S(1)}, s32[]{:T(128)}) while((s32[]{:T(128)}, f32[2,2,4116]{2,1,0:T(2,128)S(1)}, s32[8,3]{0,1:T(4,128)S(1)}, f32[8,2,4097]{2,1,0:T(2,128)S(1)}, s32[]{:T(128)}) %tuple.227), condition=%wide.while_cond.3, body=%wide.while_body.3.sunk | while | flops 2 | bytes 67701 | solution.py:53
  1098.6 16.3 %while.75 = (s32[]{:T(128)}, f32[2,2,4116]{2,1,0:T(2,128)S(1)}, s32[8,3]{0,1:T(4,128)S(1)}, f32[8,2,4097]{2,1,0:T(2,128)S(1)}, s32[]{:T(128)}) while((s32[]{:T(128)}, f32[2,2,4116]{2,1,0:T(2,128)S(1)}, s32[8,3]{0,1:T(4,128)S(1)}, f32[8,2,4097]{2,1,0:T(2,128)S(1)}, s32[]{:T(128)}) %tuple.227), condition=%wide.while_cond.3, body=%wide.while_body.3.sunk | while | flops 2 | bytes 67701 | solution.py:53
  1115.7 16.3 %while.75 = (s32[]{:T(128)}, f32[2,2,4116]{2,1,0:T(2,128)S(1)}, s32[8,3]{0,1:T(4,128)S(1)}, f32[8,2,4097]{2,1,0:T(2,128)S(1)}, s32[]{:T(128)}) while((s32[]{:T(128)}, f32[2,2,4116]{2,1,0:T(2,128)S(1)}, s32[8,3]{0,1:T(4,128)S(1)}, f32[8,2,4097]{2,1,0:T(2,128)S(1)}, s32[]{:T(128)}) %tuple.227), condition=%wide.while_cond.3, body=%wide.while_body.3.sunk | while | flops 2 | bytes 67701 | solution.py:53
  1132.9 16.3 %while.75 = (s32[]{:T(128)}, f32[2,2,4116]{2,1,0:T(2,128)S(1)}, s32[8,3]{0,1:T(4,128)S(1)}, f32[8,2,4097]{2,1,0:T(2,128)S(1)}, s32[]{:T(128)}) while((s32[]{:T(128)}, f32[2,2,4116]{2,1,0:T(2,128)S(1)}, s32[8,3]{0,1:T(4,128)S(1)}, f32[8,2,4097]{2,1,0:T(2,128)S(1)}, s32[]{:T(128)}) %tuple.227), condition=%wide.while_cond.3, body=%wide.while_body.3.sunk | while | flops 2 | bytes 67701 | solution.py:53
  1150.0 16.3 %while.75 = (s32[]{:T(128)}, f32[2,2,4116]{2,1,0:T(2,128)S(1)}, s32[8,3]{0,1:T(4,128)S(1)}, f32[8,2,4097]{2,1,0:T(2,128)S(1)}, s32[]{:T(128)}) while((s32[]{:T(128)}, f32[2,2,4116]{2,1,0:T(2,128)S(1)}, s32[8,3]{0,1:T(4,128)S(1)}, f32[8,2,4097]{2,1,0:T(2,128)S(1)}, s32[]{:T(128)}) %tuple.227), condition=%wide.while_cond.3, body=%wide.while_body.3.sunk | while | flops 2 | bytes 67701 | solution.py:53
  1167.2 16.3 %while.75 = (s32[]{:T(128)}, f32[2,2,4116]{2,1,0:T(2,128)S(1)}, s32[8,3]{0,1:T(4,128)S(1)}, f32[8,2,4097]{2,1,0:T(2,128)S(1)}, s32[]{:T(128)}) while((s32[]{:T(128)}, f32[2,2,4116]{2,1,0:T(2,128)S(1)}, s32[8,3]{0,1:T(4,128)S(1)}, f32[8,2,4097]{2,1,0:T(2,128)S(1)}, s32[]{:T(128)}) %tuple.227), condition=%wide.while_cond.3, body=%wide.while_body.3.sunk | while | flops 2 | bytes 67701 | solution.py:53
  1184.3 16.3 %while.75 = (s32[]{:T(128)}, f32[2,2,4116]{2,1,0:T(2,128)S(1)}, s32[8,3]{0,1:T(4,128)S(1)}, f32[8,2,4097]{2,1,0:T(2,128)S(1)}, s32[]{:T(128)}) while((s32[]{:T(128)}, f32[2,2,4116]{2,1,0:T(2,128)S(1)}, s32[8,3]{0,1:T(4,128)S(1)}, f32[8,2,4097]{2,1,0:T(2,128)S(1)}, s32[]{:T(128)}) %tuple.227), condition=%wide.while_cond.3, body=%wide.while_body.3.sunk | while | flops 2 | bytes 67701 | solution.py:53
  1201.5 16.3 %while.75 = (s32[]{:T(128)}, f32[2,2,4116]{2,1,0:T(2,128)S(1)}, s32[8,3]{0,1:T(4,128)S(1)}, f32[8,2,4097]{2,1,0:T(2,128)S(1)}, s32[]{:T(128)}) while((s32[]{:T(128)}, f32[2,2,4116]{2,1,0:T(2,128)S(1)}, s32[8,3]{0,1:T(4,128)S(1)}, f32[8,2,4097]{2,1,0:T(2,128)S(1)}, s32[]{:T(128)}) %tuple.227), condition=%wide.while_cond.3, body=%wide.while_body.3.sunk | while | flops 2 | bytes 67701 | solution.py:53
  1218.6 16.3 %while.75 = (s32[]{:T(128)}, f32[2,2,4116]{2,1,0:T(2,128)S(1)}, s32[8,3]{0,1:T(4,128)S(1)}, f32[8,2,4097]{2,1,0:T(2,128)S(1)}, s32[]{:T(128)}) while((s32[]{:T(128)}, f32[2,2,4116]{2,1,0:T(2,128)S(1)}, s32[8,3]{0,1:T(4,128)S(1)}, f32[8,2,4097]{2,1,0:T(2,128)S(1)}, s32[]{:T(128)}) %tuple.227), condition=%wide.while_cond.3, body=%wide.while_body.3.sunk | while | flops 2 | bytes 67701 | solution.py:53
  1235.8 16.3 %while.75 = (s32[]{:T(128)}, f32[2,2,4116]{2,1,0:T(2,128)S(1)}, s32[8,3]{0,1:T(4,128)S(1)}, f32[8,2,4097]{2,1,0:T(2,128)S(1)}, s32[]{:T(128)}) while((s32[]{:T(128)}, f32[2,2,4116]{2,1,0:T(2,128)S(1)}, s32[8,3]{0,1:T(4,128)S(1)}, f32[8,2,4097]{2,1,0:T(2,128)S(1)}, s32[]{:T(128)}) %tuple.227), condition=%wide.while_cond.3, body=%wide.while_body.3.sunk | while | flops 2 | bytes 67701 | solution.py:53
  1252.9 16.3 %while.75 = (s32[]{:T(128)}, f32[2,2,4116]{2,1,0:T(2,128)S(1)}, s32[8,3]{0,1:T(4,128)S(1)}, f32[8,2,4097]{2,1,0:T(2,128)S(1)}, s32[]{:T(128)}) while((s32[]{:T(128)}, f32[2,2,4116]{2,1,0:T(2,128)S(1)}, s32[8,3]{0,1:T(4,128)S(1)}, f32[8,2,4097]{2,1,0:T(2,128)S(1)}, s32[]{:T(128)}) %tuple.227), condition=%wide.while_cond.3, body=%wide.while_body.3.sunk | while | flops 2 | bytes 67701 | solution.py:53
  1270.1 16.3 %while.75 = (s32[]{:T(128)}, f32[2,2,4116]{2,1,0:T(2,128)S(1)}, s32[8,3]{0,1:T(4,128)S(1)}, f32[8,2,4097]{2,1,0:T(2,128)S(1)}, s32[]{:T(128)}) while((s32[]{:T(128)}, f32[2,2,4116]{2,1,0:T(2,128)S(1)}, s32[8,3]{0,1:T(4,128)S(1)}, f32[8,2,4097]{2,1,0:T(2,128)S(1)}, s32[]{:T(128)}) %tuple.227), condition=%wide.while_cond.3, body=%wide.while_body.3.sunk | while | flops 2 | bytes 67701 | solution.py:53
  1287.2 16.3 %while.75 = (s32[]{:T(128)}, f32[2,2,4116]{2,1,0:T(2,128)S(1)}, s32[8,3]{0,1:T(4,128)S(1)}, f32[8,2,4097]{2,1,0:T(2,128)S(1)}, s32[]{:T(128)}) while((s32[]{:T(128)}, f32[2,2,4116]{2,1,0:T(2,128)S(1)}, s32[8,3]{0,1:T(4,128)S(1)}, f32[8,2,4097]{2,1,0:T(2,128)S(1)}, s32[]{:T(128)}) %tuple.227), condition=%wide.while_cond.3, body=%wide.while_body.3.sunk | while | flops 2 | bytes 67701 | solution.py:53
  (2214 shorter events, 1561.6 us)
Async XLA Ops:
  6.5 317.9 %all-reduce.21.cloned.1.call-start = ((), (), s32[]{:S(2)}) async-start(), calls=%async_computation | async-start | bytes 2097152 | tf_op jit(solution)/shard_map/psum | solution.py:149
  285.3 1.0 copy-start.1
  285.3 39.1 %copy-start = (f32[1,32,2,4096]{3,2,1,0:T(2,128)S(1)}, f32[1,32,2,4096]{3,2,1,0:T(2,128)}, u32[]{:S(2)}) copy-start(f32[1,32,2,4096]{3,2,1,0:T(2,128)} %param.13) | copy-start | bytes 3145732
  286.3 78.0 %all-reduce.23.cloned.1.call-start = ((), (), s32[]{:S(2)}) async-start(), calls=%async_computation.1 | async-start | bytes 2097152 | tf_op jit(solution)/shard_map/psum | solution.py:16
  327.4 660.2 %all-reduce.25.cloned.1.call-start = ((), (), s32[]{:S(2)}) async-start(), calls=%async_computation.2 | async-start | bytes 2097152 | tf_op jit(solution)/shard_map/psum | solution.py:149
  366.7 274.4 %copy-start.3 = (f32[2,4,4096]{2,1,0:T(4,128)S(1)}, f32[2,4,4096]{2,1,0:T(4,128)}, u32[]{:S(2)}) copy-start(f32[2,4,4096]{2,1,0:T(4,128)} %param.12) | copy-start | bytes 393220
  641.2 5.6 collective-permute-start
  644.8 5.2 collective-permute-start.1
  650.2 5.0 collective-permute-start.2
  653.3 5.7 collective-permute-start.3
  659.9 5.3 collective-permute-start.4
  663.3 5.2 collective-permute-start.5
  668.6 5.9 collective-permute-start.6
  672.6 5.7 collective-permute-start.7
  950.9 1.0 copy-start.2
  951.9 75.6 %all-reduce.27.cloned.1.call-start = ((), (), s32[]{:S(2)}) async-start(), calls=%async_computation.3 | async-start | bytes 2097152 | tf_op jit(solution)/shard_map/psum | solution.py:16
  1304.4 5.5 collective-permute-start.8
  1307.9 5.2 collective-permute-start.9
  1313.3 5.0 collective-permute-start.10
  1316.4 5.7 collective-permute-start.11
  1323.1 5.3 collective-permute-start.12
  1326.4 5.2 collective-permute-start.13
  1331.7 5.9 collective-permute-start.14
  1335.8 5.7 collective-permute-start.15
Sparse Core Ops, SparseCore 0:
  286.4 37.9 all-reduce.20
  327.5 36.7 all-reduce.22
  952.0 35.5 all-reduce.24
  990.6 36.7 all-reduce.26
where the time goes:
time: 1360 us; the launch traced here: 1350 us
  local copies, waits for them, and re-layouts  1050 us (77%)
  waiting for transfers between devices  176 us (13%)
  other arithmetic  47.8 us (4%)
  starting transfers between devices  41 us (3%)
  between operations  18.7 us (1%)
  loops' own time  14.7 us (1%)
    gather x1536, local copies, waits for them, and re-layouts  1030 us
    psum x2, waiting for transfers between devices, broadcast(): return lax.psum(kept, axis)  73.6 us
    psum x2, waiting for transfers between devices, on_device(): totals = lax.psum(partial_value, 'ray')  72.5 us
    ppermute x8, starting transfers between devices, padded_2(): lax.ppermute(lax.slice_in_dim(block, block.shape[dim] - width, None, axis...  28 us
    ppermute x8, waiting for transfers between devices, padded_2(): lax.ppermute(lax.slice_in_dim(block, 0, width, axis=dim), axis, backward)  27.3 us
  transfers between devices with their start and end apart: 20, of which 16 were waited for; matrix products, arithmetic and copies ran while one was open for 0% of the time, Pallas kernels for 0%

commit v1 on v0

--- a/solution.py
+++ b/solution.py
@@ -146,7 +146,9 @@
         )
         padded = jnp.pad(current, ((0, 0), (0, 0), (margin, margin)))
         partial_value = project_block(padded, shifts, fraction, margin, breadth)
-        totals = lax.psum(partial_value, "ray")
+        totals = partial_value
+        for hop in (1, 2):
+            totals = totals + lax.ppermute(totals, "ray", [(dev, dev ^ hop) for dev in range(4)])
         residual = broadcast(stored - totals, "ray", subset_slot)
         res_padded = jnp.pad(residual, ((0, 0), (0, 0), (margin, margin)))
         current = current + back_block(res_padded, shifts, fraction, margin, breadth) / (

time: 1360 us -> 1310 us (0.963)
  local copies, waits for them, and re-layouts: 1050 us -> 1020 us
  waiting for transfers between devices: 176 us -> 154 us
    psum x2 -> x0, waiting for transfers between devices: 72.5 us -> none  [on_device(): totals = lax.psum(partial_value, 'ray')]
    ppermute x0 -> x4, waiting for transfers between devices: none -> 50.7 us  [on_device(): lax.ppermute(totals, 'ray', [(dev, dev ^ hop) for dev in range(4)])]
    gather x1536, local copies, waits for them, and re-layouts: 1030 us -> 1000 us
  transfers between devices with their start and end apart: 20 -> 22, of which waited for: 16 -> 18; matrix products, arithmetic and copies ran while one was open for 0% -> 0% of each run, Pallas kernels for 0% -> 0%
where the time goes in v1:
time: 1310 us; the launch traced here: 1300 us
  local copies, waits for them, and re-layouts  1020 us (78%)
  waiting for transfers between devices  154 us (12%)
  other arithmetic  47.5 us (4%)
  starting transfers between devices  44.9 us (3%)
  between operations  18.5 us (1%)
  loops' own time  14.7 us (1%)
    gather x1536, local copies, waits for them, and re-layouts  1000 us
    psum x2, waiting for transfers between devices, broadcast(): return lax.psum(kept, axis)  74 us
    ppermute x4, waiting for transfers between devices, on_device(): lax.ppermute(totals, 'ray', [(dev, dev ^ hop) for dev in range(4)])  50.7 us
    ppermute x8, starting transfers between devices, padded_2(): lax.ppermute(lax.slice_in_dim(block, block.shape[dim] - width, None, axis...  28 us
    ppermute x8, waiting for transfers between devices, padded_2(): lax.ppermute(lax.slice_in_dim(block, 0, width, axis=dim), axis, backward)  27.3 us
  transfers between devices with their start and end apart: 22, of which 18 were waited for; matrix products, arithmetic and copies ran while one was open for 0% of the time, Pallas kernels for 0%

profile of v1, /device:TPU:1, one launch (start us, length us, event | category | flops | bytes accessed | tf_op | source)
XLA Modules:
  0.0 1296.9 jit_solution(6927985895491483402)
XLA Ops:
  14.1 267.2 %while.65 = (s32[]{:T(128)}, f32[16,2,2,4096]{3,2,1,0:T(2,128)S(1)}, f32[16,2,4]{2,1,0:T(2,128)S(1)}, f32[2,4,4116]{2,0,1:T(2,128)S(1)}, s32[16,2,4]{2,1,0:T(2,128)S(1)}, /*index=5*/s32[]{:T(128)}, s32[]{:T(128)}, s32[]{:T(128)}) while((s32[]{:T(128)}, f32[16,2,2,4096]{3,2,1,0:T(2,128)S(1)}, f32[16,2,4]{2,1,0:T(2,128)S(1)}, ...), condition=%wide.region_2.3_spmd, body=%wide.region_0.2_spmd.sunk | while | flops 245828 | bytes 789350 | solution.py:70
  14.2 16.1 %while.72 = (s32[]{:T(128)}, f32[4,2,4116]{2,1,0:T(2,128)S(1)}, s32[8,3]{0,1:T(4,128)S(1)}, f32[8,2,4097]{2,1,0:T(2,128)S(1)}, s32[]{:T(128)}) while((s32[]{:T(128)}, f32[4,2,4116]{2,1,0:T(2,128)S(1)}, s32[8,3]{0,1:T(4,128)S(1)}, f32[8,2,4097]{2,1,0:T(2,128)S(1)}, s32[]{:T(128)}) %tuple.255), condition=%wide.while_cond, body=%wide.while_body.sunk | while | flops 2 | bytes 67701 | solution.py:45
  30.9 16.1 %while.72 = (s32[]{:T(128)}, f32[4,2,4116]{2,1,0:T(2,128)S(1)}, s32[8,3]{0,1:T(4,128)S(1)}, f32[8,2,4097]{2,1,0:T(2,128)S(1)}, s32[]{:T(128)}) while((s32[]{:T(128)}, f32[4,2,4116]{2,1,0:T(2,128)S(1)}, s32[8,3]{0,1:T(4,128)S(1)}, f32[8,2,4097]{2,1,0:T(2,128)S(1)}, s32[]{:T(128)}) %tuple.255), condition=%wide.while_cond, body=%wide.while_body.sunk | while | flops 2 | bytes 67701 | solution.py:45
  47.6 16.1 %while.72 = (s32[]{:T(128)}, f32[4,2,4116]{2,1,0:T(2,128)S(1)}, s32[8,3]{0,1:T(4,128)S(1)}, f32[8,2,4097]{2,1,0:T(2,128)S(1)}, s32[]{:T(128)}) while((s32[]{:T(128)}, f32[4,2,4116]{2,1,0:T(2,128)S(1)}, s32[8,3]{0,1:T(4,128)S(1)}, f32[8,2,4097]{2,1,0:T(2,128)S(1)}, s32[]{:T(128)}) %tuple.255), condition=%wide.while_cond, body=%wide.while_body.sunk | while | flops 2 | bytes 67701 | solution.py:45
  64.3 16.1 %while.72 = (s32[]{:T(128)}, f32[4,2,4116]{2,1,0:T(2,128)S(1)}, s32[8,3]{0,1:T(4,128)S(1)}, f32[8,2,4097]{2,1,0:T(2,128)S(1)}, s32[]{:T(128)}) while((s32[]{:T(128)}, f32[4,2,4116]{2,1,0:T(2,128)S(1)}, s32[8,3]{0,1:T(4,128)S(1)}, f32[8,2,4097]{2,1,0:T(2,128)S(1)}, s32[]{:T(128)}) %tuple.255), condition=%wide.while_cond, body=%wide.while_body.sunk | while | flops 2 | bytes 67701 | solution.py:45
  81.0 16.1 %while.72 = (s32[]{:T(128)}, f32[4,2,4116]{2,1,0:T(2,128)S(1)}, s32[8,3]{0,1:T(4,128)S(1)}, f32[8,2,4097]{2,1,0:T(2,128)S(1)}, s32[]{:T(128)}) while((s32[]{:T(128)}, f32[4,2,4116]{2,1,0:T(2,128)S(1)}, s32[8,3]{0,1:T(4,128)S(1)}, f32[8,2,4097]{2,1,0:T(2,128)S(1)}, s32[]{:T(128)}) %tuple.255), condition=%wide.while_cond, body=%wide.while_body.sunk | while | flops 2 | bytes 67701 | solution.py:45
  97.7 16.1 %while.72 = (s32[]{:T(128)}, f32[4,2,4116]{2,1,0:T(2,128)S(1)}, s32[8,3]{0,1:T(4,128)S(1)}, f32[8,2,4097]{2,1,0:T(2,128)S(1)}, s32[]{:T(128)}) while((s32[]{:T(128)}, f32[4,2,4116]{2,1,0:T(2,128)S(1)}, s32[8,3]{0,1:T(4,128)S(1)}, f32[8,2,4097]{2,1,0:T(2,128)S(1)}, s32[]{:T(128)}) %tuple.255), condition=%wide.while_cond, body=%wide.while_body.sunk | while | flops 2 | bytes 67701 | solution.py:45
  114.4 16.1 %while.72 = (s32[]{:T(128)}, f32[4,2,4116]{2,1,0:T(2,128)S(1)}, s32[8,3]{0,1:T(4,128)S(1)}, f32[8,2,4097]{2,1,0:T(2,128)S(1)}, s32[]{:T(128)}) while((s32[]{:T(128)}, f32[4,2,4116]{2,1,0:T(2,128)S(1)}, s32[8,3]{0,1:T(4,128)S(1)}, f32[8,2,4097]{2,1,0:T(2,128)S(1)}, s32[]{:T(128)}) %tuple.255), condition=%wide.while_cond, body=%wide.while_body.sunk | while | flops 2 | bytes 67701 | solution.py:45
  131.1 16.1 %while.72 = (s32[]{:T(128)}, f32[4,2,4116]{2,1,0:T(2,128)S(1)}, s32[8,3]{0,1:T(4,128)S(1)}, f32[8,2,4097]{2,1,0:T(2,128)S(1)}, s32[]{:T(128)}) while((s32[]{:T(128)}, f32[4,2,4116]{2,1,0:T(2,128)S(1)}, s32[8,3]{0,1:T(4,128)S(1)}, f32[8,2,4097]{2,1,0:T(2,128)S(1)}, s32[]{:T(128)}) %tuple.255), condition=%wide.while_cond, body=%wide.while_body.sunk | while | flops 2 | bytes 67701 | solution.py:45
  147.8 16.1 %while.72 = (s32[]{:T(128)}, f32[4,2,4116]{2,1,0:T(2,128)S(1)}, s32[8,3]{0,1:T(4,128)S(1)}, f32[8,2,4097]{2,1,0:T(2,128)S(1)}, s32[]{:T(128)}) while((s32[]{:T(128)}, f32[4,2,4116]{2,1,0:T(2,128)S(1)}, s32[8,3]{0,1:T(4,128)S(1)}, f32[8,2,4097]{2,1,0:T(2,128)S(1)}, s32[]{:T(128)}) %tuple.255), condition=%wide.while_cond, body=%wide.while_body.sunk | while | flops 2 | bytes 67701 | solution.py:45
  164.5 16.1 %while.72 = (s32[]{:T(128)}, f32[4,2,4116]{2,1,0:T(2,128)S(1)}, s32[8,3]{0,1:T(4,128)S(1)}, f32[8,2,4097]{2,1,0:T(2,128)S(1)}, s32[]{:T(128)}) while((s32[]{:T(128)}, f32[4,2,4116]{2,1,0:T(2,128)S(1)}, s32[8,3]{0,1:T(4,128)S(1)}, f32[8,2,4097]{2,1,0:T(2,128)S(1)}, s32[]{:T(128)}) %tuple.255), condition=%wide.while_cond, body=%wide.while_body.sunk | while | flops 2 | bytes 67701 | solution.py:45
  181.2 16.1 %while.72 = (s32[]{:T(128)}, f32[4,2,4116]{2,1,0:T(2,128)S(1)}, s32[8,3]{0,1:T(4,128)S(1)}, f32[8,2,4097]{2,1,0:T(2,128)S(1)}, s32[]{:T(128)}) while((s32[]{:T(128)}, f32[4,2,4116]{2,1,0:T(2,128)S(1)}, s32[8,3]{0,1:T(4,128)S(1)}, f32[8,2,4097]{2,1,0:T(2,128)S(1)}, s32[]{:T(128)}) %tuple.255), condition=%wide.while_cond, body=%wide.while_body.sunk | while | flops 2 | bytes 67701 | solution.py:45
  197.9 16.1 %while.72 = (s32[]{:T(128)}, f32[4,2,4116]{2,1,0:T(2,128)S(1)}, s32[8,3]{0,1:T(4,128)S(1)}, f32[8,2,4097]{2,1,0:T(2,128)S(1)}, s32[]{:T(128)}) while((s32[]{:T(128)}, f32[4,2,4116]{2,1,0:T(2,128)S(1)}, s32[8,3]{0,1:T(4,128)S(1)}, f32[8,2,4097]{2,1,0:T(2,128)S(1)}, s32[]{:T(128)}) %tuple.255), condition=%wide.while_cond, body=%wide.while_body.sunk | while | flops 2 | bytes 67701 | solution.py:45
  214.6 16.1 %while.72 = (s32[]{:T(128)}, f32[4,2,4116]{2,1,0:T(2,128)S(1)}, s32[8,3]{0,1:T(4,128)S(1)}, f32[8,2,4097]{2,1,0:T(2,128)S(1)}, s32[]{:T(128)}) while((s32[]{:T(128)}, f32[4,2,4116]{2,1,0:T(2,128)S(1)}, s32[8,3]{0,1:T(4,128)S(1)}, f32[8,2,4097]{2,1,0:T(2,128)S(1)}, s32[]{:T(128)}) %tuple.255), condition=%wide.while_cond, body=%wide.while_body.sunk | while | flops 2 | bytes 67701 | solution.py:45
  231.3 16.1 %while.72 = (s32[]{:T(128)}, f32[4,2,4116]{2,1,0:T(2,128)S(1)}, s32[8,3]{0,1:T(4,128)S(1)}, f32[8,2,4097]{2,1,0:T(2,128)S(1)}, s32[]{:T(128)}) while((s32[]{:T(128)}, f32[4,2,4116]{2,1,0:T(2,128)S(1)}, s32[8,3]{0,1:T(4,128)S(1)}, f32[8,2,4097]{2,1,0:T(2,128)S(1)}, s32[]{:T(128)}) %tuple.255), condition=%wide.while_cond, body=%wide.while_body.sunk | while | flops 2 | bytes 67701 | solution.py:45
  248.0 16.1 %while.72 = (s32[]{:T(128)}, f32[4,2,4116]{2,1,0:T(2,128)S(1)}, s32[8,3]{0,1:T(4,128)S(1)}, f32[8,2,4097]{2,1,0:T(2,128)S(1)}, s32[]{:T(128)}) while((s32[]{:T(128)}, f32[4,2,4116]{2,1,0:T(2,128)S(1)}, s32[8,3]{0,1:T(4,128)S(1)}, f32[8,2,4097]{2,1,0:T(2,128)S(1)}, s32[]{:T(128)}) %tuple.255), condition=%wide.while_cond, body=%wide.while_body.sunk | while | flops 2 | bytes 67701 | solution.py:45
  264.7 16.1 %while.72 = (s32[]{:T(128)}, f32[4,2,4116]{2,1,0:T(2,128)S(1)}, s32[8,3]{0,1:T(4,128)S(1)}, f32[8,2,4097]{2,1,0:T(2,128)S(1)}, s32[]{:T(128)}) while((s32[]{:T(128)}, f32[4,2,4116]{2,1,0:T(2,128)S(1)}, s32[8,3]{0,1:T(4,128)S(1)}, f32[8,2,4097]{2,1,0:T(2,128)S(1)}, s32[]{:T(128)}) %tuple.255), condition=%wide.while_cond, body=%wide.while_body.sunk | while | flops 2 | bytes 67701 | solution.py:45
  287.7 22.5 %collective-permute-done.1 = f32[32,2,4096]{2,1,0:T(2,128)S(1)} collective-permute-done((f32[32,2,4096]{2,1,0:T(2,128)S(1)}, f32[32,2,4096]{2,1,0:T(2,128)S(1)}, u32[]{:S(2)}, u32[]{:S(2)}) %collective-permute-start.1) | collective-permute-done | bytes 1048608 | tf_op jit(solution)/shard_map/ppermute | solution.py:151
  312.6 37.6 %all-reduce.19.cloned.1.call-done = f32[32,2,4096]{2,1,0:T(2,128)} async-done(((f32[32,2,4096]{2,1,0:T(2,128)}), f32[32,2,4096]{2,1,0:T(2,128)}) %all-reduce.19.cloned.1.call-update) | async-done | bytes 1048592 | tf_op jit(solution)/shard_map/psum | solution.py:16
  352.7 264.7 %while.69 = (s32[]{:T(128)}, f32[2,4,4096]{2,0,1:T(2,128)S(1)}, f32[16,2,4]{2,1,0:T(2,128)S(1)}, f32[16,2,2,4116]{3,2,1,0:T(2,128)S(1)}, s32[16,2,4]{2,1,0:T(2,128)S(1)}, /*index=5*/s32[]{:T(128)}, s32[]{:T(128)}, s32[]{:T(128)}) while((s32[]{:T(128)}, f32[2,4,4096]{2,0,1:T(2,128)S(1)}, f32[16,2,4]{2,1,0:T(2,128)S(1)}, ...), condition=%wide.region_6.7_spmd.clone, body=%wide.region_4.6_spmd.clone.sunk | while | flops 294981 | bytes 1248752 | solution.py:92
  352.8 15.7 %while.74 = (s32[]{:T(128)}, f32[2,2,4116]{2,1,0:T(2,128)S(1)}, s32[8,3]{0,1:T(4,128)S(1)}, f32[8,2,4097]{2,1,0:T(2,128)S(1)}, s32[]{:T(128)}) while((s32[]{:T(128)}, f32[2,2,4116]{2,1,0:T(2,128)S(1)}, s32[8,3]{0,1:T(4,128)S(1)}, f32[8,2,4097]{2,1,0:T(2,128)S(1)}, s32[]{:T(128)}) %tuple.230), condition=%wide.while_cond.1, body=%wide.while_body.1.sunk | while | flops 2 | bytes 67701 | solution.py:53
  369.4 15.7 %while.74 = (s32[]{:T(128)}, f32[2,2,4116]{2,1,0:T(2,128)S(1)}, s32[8,3]{0,1:T(4,128)S(1)}, f32[8,2,4097]{2,1,0:T(2,128)S(1)}, s32[]{:T(128)}) while((s32[]{:T(128)}, f32[2,2,4116]{2,1,0:T(2,128)S(1)}, s32[8,3]{0,1:T(4,128)S(1)}, f32[8,2,4097]{2,1,0:T(2,128)S(1)}, s32[]{:T(128)}) %tuple.230), condition=%wide.while_cond.1, body=%wide.while_body.1.sunk | while | flops 2 | bytes 67701 | solution.py:53
  385.9 15.7 %while.74 = (s32[]{:T(128)}, f32[2,2,4116]{2,1,0:T(2,128)S(1)}, s32[8,3]{0,1:T(4,128)S(1)}, f32[8,2,4097]{2,1,0:T(2,128)S(1)}, s32[]{:T(128)}) while((s32[]{:T(128)}, f32[2,2,4116]{2,1,0:T(2,128)S(1)}, s32[8,3]{0,1:T(4,128)S(1)}, f32[8,2,4097]{2,1,0:T(2,128)S(1)}, s32[]{:T(128)}) %tuple.230), condition=%wide.while_cond.1, body=%wide.while_body.1.sunk | while | flops 2 | bytes 67701 | solution.py:53
  402.5 15.7 %while.74 = (s32[]{:T(128)}, f32[2,2,4116]{2,1,0:T(2,128)S(1)}, s32[8,3]{0,1:T(4,128)S(1)}, f32[8,2,4097]{2,1,0:T(2,128)S(1)}, s32[]{:T(128)}) while((s32[]{:T(128)}, f32[2,2,4116]{2,1,0:T(2,128)S(1)}, s32[8,3]{0,1:T(4,128)S(1)}, f32[8,2,4097]{2,1,0:T(2,128)S(1)}, s32[]{:T(128)}) %tuple.230), condition=%wide.while_cond.1, body=%wide.while_body.1.sunk | while | flops 2 | bytes 67701 | solution.py:53
  419.0 15.7 %while.74 = (s32[]{:T(128)}, f32[2,2,4116]{2,1,0:T(2,128)S(1)}, s32[8,3]{0,1:T(4,128)S(1)}, f32[8,2,4097]{2,1,0:T(2,128)S(1)}, s32[]{:T(128)}) while((s32[]{:T(128)}, f32[2,2,4116]{2,1,0:T(2,128)S(1)}, s32[8,3]{0,1:T(4,128)S(1)}, f32[8,2,4097]{2,1,0:T(2,128)S(1)}, s32[]{:T(128)}) %tuple.230), condition=%wide.while_cond.1, body=%wide.while_body.1.sunk | while | flops 2 | bytes 67701 | solution.py:53
  435.5 15.7 %while.74 = (s32[]{:T(128)}, f32[2,2,4116]{2,1,0:T(2,128)S(1)}, s32[8,3]{0,1:T(4,128)S(1)}, f32[8,2,4097]{2,1,0:T(2,128)S(1)}, s32[]{:T(128)}) while((s32[]{:T(128)}, f32[2,2,4116]{2,1,0:T(2,128)S(1)}, s32[8,3]{0,1:T(4,128)S(1)}, f32[8,2,4097]{2,1,0:T(2,128)S(1)}, s32[]{:T(128)}) %tuple.230), condition=%wide.while_cond.1, body=%wide.while_body.1.sunk | while | flops 2 | bytes 67701 | solution.py:53
  452.1 15.7 %while.74 = (s32[]{:T(128)}, f32[2,2,4116]{2,1,0:T(2,128)S(1)}, s32[8,3]{0,1:T(4,128)S(1)}, f32[8,2,4097]{2,1,0:T(2,128)S(1)}, s32[]{:T(128)}) while((s32[]{:T(128)}, f32[2,2,4116]{2,1,0:T(2,128)S(1)}, s32[8,3]{0,1:T(4,128)S(1)}, f32[8,2,4097]{2,1,0:T(2,128)S(1)}, s32[]{:T(128)}) %tuple.230), condition=%wide.while_cond.1, body=%wide.while_body.1.sunk | while | flops 2 | bytes 67701 | solution.py:53
  468.6 15.7 %while.74 = (s32[]{:T(128)}, f32[2,2,4116]{2,1,0:T(2,128)S(1)}, s32[8,3]{0,1:T(4,128)S(1)}, f32[8,2,4097]{2,1,0:T(2,128)S(1)}, s32[]{:T(128)}) while((s32[]{:T(128)}, f32[2,2,4116]{2,1,0:T(2,128)S(1)}, s32[8,3]{0,1:T(4,128)S(1)}, f32[8,2,4097]{2,1,0:T(2,128)S(1)}, s32[]{:T(128)}) %tuple.230), condition=%wide.while_cond.1, body=%wide.while_body.1.sunk | while | flops 2 | bytes 67701 | solution.py:53
  485.2 15.7 %while.74 = (s32[]{:T(128)}, f32[2,2,4116]{2,1,0:T(2,128)S(1)}, s32[8,3]{0,1:T(4,128)S(1)}, f32[8,2,4097]{2,1,0:T(2,128)S(1)}, s32[]{:T(128)}) while((s32[]{:T(128)}, f32[2,2,4116]{2,1,0:T(2,128)S(1)}, s32[8,3]{0,1:T(4,128)S(1)}, f32[8,2,4097]{2,1,0:T(2,128)S(1)}, s32[]{:T(128)}) %tuple.230), condition=%wide.while_cond.1, body=%wide.while_body.1.sunk | while | flops 2 | bytes 67701 | solution.py:53
  501.7 15.7 %while.74 = (s32[]{:T(128)}, f32[2,2,4116]{2,1,0:T(2,128)S(1)}, s32[8,3]{0,1:T(4,128)S(1)}, f32[8,2,4097]{2,1,0:T(2,128)S(1)}, s32[]{:T(128)}) while((s32[]{:T(128)}, f32[2,2,4116]{2,1,0:T(2,128)S(1)}, s32[8,3]{0,1:T(4,128)S(1)}, f32[8,2,4097]{2,1,0:T(2,128)S(1)}, s32[]{:T(128)}) %tuple.230), condition=%wide.while_cond.1, body=%wide.while_body.1.sunk | while | flops 2 | bytes 67701 | solution.py:53
  518.3 15.7 %while.74 = (s32[]{:T(128)}, f32[2,2,4116]{2,1,0:T(2,128)S(1)}, s32[8,3]{0,1:T(4,128)S(1)}, f32[8,2,4097]{2,1,0:T(2,128)S(1)}, s32[]{:T(128)}) while((s32[]{:T(128)}, f32[2,2,4116]{2,1,0:T(2,128)S(1)}, s32[8,3]{0,1:T(4,128)S(1)}, f32[8,2,4097]{2,1,0:T(2,128)S(1)}, s32[]{:T(128)}) %tuple.230), condition=%wide.while_cond.1, body=%wide.while_body.1.sunk | while | flops 2 | bytes 67701 | solution.py:53
  534.8 15.7 %while.74 = (s32[]{:T(128)}, f32[2,2,4116]{2,1,0:T(2,128)S(1)}, s32[8,3]{0,1:T(4,128)S(1)}, f32[8,2,4097]{2,1,0:T(2,128)S(1)}, s32[]{:T(128)}) while((s32[]{:T(128)}, f32[2,2,4116]{2,1,0:T(2,128)S(1)}, s32[8,3]{0,1:T(4,128)S(1)}, f32[8,2,4097]{2,1,0:T(2,128)S(1)}, s32[]{:T(128)}) %tuple.230), condition=%wide.while_cond.1, body=%wide.while_body.1.sunk | while | flops 2 | bytes 67701 | solution.py:53
  551.4 15.7 %while.74 = (s32[]{:T(128)}, f32[2,2,4116]{2,1,0:T(2,128)S(1)}, s32[8,3]{0,1:T(4,128)S(1)}, f32[8,2,4097]{2,1,0:T(2,128)S(1)}, s32[]{:T(128)}) while((s32[]{:T(128)}, f32[2,2,4116]{2,1,0:T(2,128)S(1)}, s32[8,3]{0,1:T(4,128)S(1)}, f32[8,2,4097]{2,1,0:T(2,128)S(1)}, s32[]{:T(128)}) %tuple.230), condition=%wide.while_cond.1, body=%wide.while_body.1.sunk | while | flops 2 | bytes 67701 | solution.py:53
  584.5 15.7 %while.74 = (s32[]{:T(128)}, f32[2,2,4116]{2,1,0:T(2,128)S(1)}, s32[8,3]{0,1:T(4,128)S(1)}, f32[8,2,4097]{2,1,0:T(2,128)S(1)}, s32[]{:T(128)}) while((s32[]{:T(128)}, f32[2,2,4116]{2,1,0:T(2,128)S(1)}, s32[8,3]{0,1:T(4,128)S(1)}, f32[8,2,4097]{2,1,0:T(2,128)S(1)}, s32[]{:T(128)}) %tuple.230), condition=%wide.while_cond.1, body=%wide.while_body.1.sunk | while | flops 2 | bytes 67701 | solution.py:53
  656.4 261.2 %while.67 = (s32[]{:T(128)}, f32[16,2,2,4096]{3,2,1,0:T(2,128)S(1)}, f32[16,2,4]{2,1,0:T(2,128)S(1)}, f32[2,4,4116]{2,0,1:T(2,128)S(1)}, s32[16,2,4]{2,1,0:T(2,128)S(1)}, /*index=5*/s32[]{:T(128)}, s32[]{:T(128)}, s32[]{:T(128)}) while((s32[]{:T(128)}, f32[16,2,2,4096]{3,2,1,0:T(2,128)S(1)}, f32[16,2,4]{2,1,0:T(2,128)S(1)}, ...), condition=%wide.region_9.10_spmd, body=%wide.region_7.9_spmd.sunk | while | flops 245828 | bytes 789350 | solution.py:70
  922.7 22.9 %collective-permute-done.11 = f32[32,2,4096]{2,1,0:T(2,128)S(1)} collective-permute-done((f32[32,2,4096]{2,1,0:T(2,128)S(1)}, f32[32,2,4096]{2,1,0:T(2,128)S(1)}, u32[]{:S(2)}, u32[]{:S(2)}) %collective-permute-start.11) | collective-permute-done | bytes 1048608 | tf_op jit(solution)/shard_map/ppermute | solution.py:151
  947.8 36.4 %all-reduce.21.cloned.1.call-done = f32[32,2,4096]{2,1,0:T(2,128)} async-done(((f32[32,2,4096]{2,1,0:T(2,128)}), f32[32,2,4096]{2,1,0:T(2,128)}) %all-reduce.21.cloned.1.call-update) | async-done | bytes 1048592 | tf_op jit(solution)/shard_map/psum | solution.py:16
  986.5 264.7 %while.71 = (s32[]{:T(128)}, f32[2,4,4096]{2,0,1:T(2,128)S(1)}, f32[16,2,4]{2,1,0:T(2,128)S(1)}, f32[16,2,2,4116]{3,2,1,0:T(2,128)S(1)}, s32[16,2,4]{2,1,0:T(2,128)S(1)}, /*index=5*/s32[]{:T(128)}, s32[]{:T(128)}, s32[]{:T(128)}) while((s32[]{:T(128)}, f32[2,4,4096]{2,0,1:T(2,128)S(1)}, f32[16,2,4]{2,1,0:T(2,128)S(1)}, ...), condition=%wide.region_13.14_spmd.clone, body=%wide.region_11.13_spmd.clone.sunk | while | flops 294981 | bytes 1248752 | solution.py:92
  986.7 15.7 %while.75 = (s32[]{:T(128)}, f32[2,2,4116]{2,1,0:T(2,128)S(1)}, s32[8,3]{0,1:T(4,128)S(1)}, f32[8,2,4097]{2,1,0:T(2,128)S(1)}, s32[]{:T(128)}) while((s32[]{:T(128)}, f32[2,2,4116]{2,1,0:T(2,128)S(1)}, s32[8,3]{0,1:T(4,128)S(1)}, f32[8,2,4097]{2,1,0:T(2,128)S(1)}, s32[]{:T(128)}) %tuple.227), condition=%wide.while_cond.3, body=%wide.while_body.3.sunk | while | flops 2 | bytes 67701 | solution.py:53
  1019.8 15.7 %while.75 = (s32[]{:T(128)}, f32[2,2,4116]{2,1,0:T(2,128)S(1)}, s32[8,3]{0,1:T(4,128)S(1)}, f32[8,2,4097]{2,1,0:T(2,128)S(1)}, s32[]{:T(128)}) while((s32[]{:T(128)}, f32[2,2,4116]{2,1,0:T(2,128)S(1)}, s32[8,3]{0,1:T(4,128)S(1)}, f32[8,2,4097]{2,1,0:T(2,128)S(1)}, s32[]{:T(128)}) %tuple.227), condition=%wide.while_cond.3, body=%wide.while_body.3.sunk | while | flops 2 | bytes 67701 | solution.py:53
  1036.3 15.7 %while.75 = (s32[]{:T(128)}, f32[2,2,4116]{2,1,0:T(2,128)S(1)}, s32[8,3]{0,1:T(4,128)S(1)}, f32[8,2,4097]{2,1,0:T(2,128)S(1)}, s32[]{:T(128)}) while((s32[]{:T(128)}, f32[2,2,4116]{2,1,0:T(2,128)S(1)}, s32[8,3]{0,1:T(4,128)S(1)}, f32[8,2,4097]{2,1,0:T(2,128)S(1)}, s32[]{:T(128)}) %tuple.227), condition=%wide.while_cond.3, body=%wide.while_body.3.sunk | while | flops 2 | bytes 67701 | solution.py:53
  1052.9 15.7 %while.75 = (s32[]{:T(128)}, f32[2,2,4116]{2,1,0:T(2,128)S(1)}, s32[8,3]{0,1:T(4,128)S(1)}, f32[8,2,4097]{2,1,0:T(2,128)S(1)}, s32[]{:T(128)}) while((s32[]{:T(128)}, f32[2,2,4116]{2,1,0:T(2,128)S(1)}, s32[8,3]{0,1:T(4,128)S(1)}, f32[8,2,4097]{2,1,0:T(2,128)S(1)}, s32[]{:T(128)}) %tuple.227), condition=%wide.while_cond.3, body=%wide.while_body.3.sunk | while | flops 2 | bytes 67701 | solution.py:53
  1069.4 15.7 %while.75 = (s32[]{:T(128)}, f32[2,2,4116]{2,1,0:T(2,128)S(1)}, s32[8,3]{0,1:T(4,128)S(1)}, f32[8,2,4097]{2,1,0:T(2,128)S(1)}, s32[]{:T(128)}) while((s32[]{:T(128)}, f32[2,2,4116]{2,1,0:T(2,128)S(1)}, s32[8,3]{0,1:T(4,128)S(1)}, f32[8,2,4097]{2,1,0:T(2,128)S(1)}, s32[]{:T(128)}) %tuple.227), condition=%wide.while_cond.3, body=%wide.while_body.3.sunk | while | flops 2 | bytes 67701 | solution.py:53
  1102.5 15.7 %while.75 = (s32[]{:T(128)}, f32[2,2,4116]{2,1,0:T(2,128)S(1)}, s32[8,3]{0,1:T(4,128)S(1)}, f32[8,2,4097]{2,1,0:T(2,128)S(1)}, s32[]{:T(128)}) while((s32[]{:T(128)}, f32[2,2,4116]{2,1,0:T(2,128)S(1)}, s32[8,3]{0,1:T(4,128)S(1)}, f32[8,2,4097]{2,1,0:T(2,128)S(1)}, s32[]{:T(128)}) %tuple.227), condition=%wide.while_cond.3, body=%wide.while_body.3.sunk | while | flops 2 | bytes 67701 | solution.py:53
  1135.6 15.7 %while.75 = (s32[]{:T(128)}, f32[2,2,4116]{2,1,0:T(2,128)S(1)}, s32[8,3]{0,1:T(4,128)S(1)}, f32[8,2,4097]{2,1,0:T(2,128)S(1)}, s32[]{:T(128)}) while((s32[]{:T(128)}, f32[2,2,4116]{2,1,0:T(2,128)S(1)}, s32[8,3]{0,1:T(4,128)S(1)}, f32[8,2,4097]{2,1,0:T(2,128)S(1)}, s32[]{:T(128)}) %tuple.227), condition=%wide.while_cond.3, body=%wide.while_body.3.sunk | while | flops 2 | bytes 67701 | solution.py:53
  1168.7 15.7 %while.75 = (s32[]{:T(128)}, f32[2,2,4116]{2,1,0:T(2,128)S(1)}, s32[8,3]{0,1:T(4,128)S(1)}, f32[8,2,4097]{2,1,0:T(2,128)S(1)}, s32[]{:T(128)}) while((s32[]{:T(128)}, f32[2,2,4116]{2,1,0:T(2,128)S(1)}, s32[8,3]{0,1:T(4,128)S(1)}, f32[8,2,4097]{2,1,0:T(2,128)S(1)}, s32[]{:T(128)}) %tuple.227), condition=%wide.while_cond.3, body=%wide.while_body.3.sunk | while | flops 2 | bytes 67701 | solution.py:53
  1201.8 15.7 %while.75 = (s32[]{:T(128)}, f32[2,2,4116]{2,1,0:T(2,128)S(1)}, s32[8,3]{0,1:T(4,128)S(1)}, f32[8,2,4097]{2,1,0:T(2,128)S(1)}, s32[]{:T(128)}) while((s32[]{:T(128)}, f32[2,2,4116]{2,1,0:T(2,128)S(1)}, s32[8,3]{0,1:T(4,128)S(1)}, f32[8,2,4097]{2,1,0:T(2,128)S(1)}, s32[]{:T(128)}) %tuple.227), condition=%wide.while_cond.3, body=%wide.while_body.3.sunk | while | flops 2 | bytes 67701 | solution.py:53
  1234.9 15.7 %while.75 = (s32[]{:T(128)}, f32[2,2,4116]{2,1,0:T(2,128)S(1)}, s32[8,3]{0,1:T(4,128)S(1)}, f32[8,2,4097]{2,1,0:T(2,128)S(1)}, s32[]{:T(128)}) while((s32[]{:T(128)}, f32[2,2,4116]{2,1,0:T(2,128)S(1)}, s32[8,3]{0,1:T(4,128)S(1)}, f32[8,2,4097]{2,1,0:T(2,128)S(1)}, s32[]{:T(128)}) %tuple.227), condition=%wide.while_cond.3, body=%wide.while_body.3.sunk | while | flops 2 | bytes 67701 | solution.py:53
  (2214 shorter events, 1521.4 us)
Async XLA Ops:
  6.5 343.7 %all-reduce.19.cloned.1.call-start = ((), (), s32[]{:S(2)}) async-start(), calls=%async_computation | async-start | bytes 2097152 | tf_op jit(solution)/shard_map/psum | solution.py:16
  281.3 29.0 %copy-start = (f32[1,32,2,4096]{3,2,1,0:T(2,128)S(1)}, f32[1,32,2,4096]{3,2,1,0:T(2,128)}, u32[]{:S(2)}) copy-start(f32[1,32,2,4096]{3,2,1,0:T(2,128)} %param.13) | copy-start | bytes 3145732
  281.3 2.7 collective-permute-start
  284.7 25.6 %collective-permute-start.1 = (f32[32,2,4096]{2,1,0:T(2,128)S(1)}, f32[32,2,4096]{2,1,0:T(2,128)S(1)}, u32[]{:S(2)}, u32[]{:S(2)}) collective-permute-start(f32[32,2,4096]{2,1,0:T(2,128)S(1)} %bitcast_add_fusion.1), channel_id=1, source_target_pairs={{0,16},{8,24},{16,0},{24,8},{1,17},{9,25},{17,1},{25,9},{2,18},{10... | collective-permute-start | bytes 3145736 | tf_op jit(solution)/shard_map/ppermute | solution.py:151
  312.4 671.7 %all-reduce.21.cloned.1.call-start = ((), (), s32[]{:S(2)}) async-start(), calls=%async_computation.1 | async-start | bytes 2097152 | tf_op jit(solution)/shard_map/psum | solution.py:16
  352.6 264.8 %copy-start.1 = (f32[2,4,4096]{2,1,0:T(4,128)S(1)}, f32[2,4,4096]{2,1,0:T(4,128)}, u32[]{:S(2)}) copy-start(f32[2,4,4096]{2,1,0:T(4,128)} %param.12) | copy-start | bytes 393220
  617.6 5.6 collective-permute-start.2
  621.2 5.2 collective-permute-start.3
  626.5 5.0 collective-permute-start.4
  629.6 5.7 collective-permute-start.5
  636.3 5.3 collective-permute-start.6
  639.6 5.2 collective-permute-start.7
  645.0 5.9 collective-permute-start.8
  649.0 5.7 collective-permute-start.9
  917.6 2.7 collective-permute-start.10
  920.9 24.6 %collective-permute-start.11 = (f32[32,2,4096]{2,1,0:T(2,128)S(1)}, f32[32,2,4096]{2,1,0:T(2,128)S(1)}, u32[]{:S(2)}, u32[]{:S(2)}) collective-permute-start(f32[32,2,4096]{2,1,0:T(2,128)S(1)} %bitcast_add_fusion), channel_id=1, source_target_pairs={{0,16},{8,24},{16,0},{24,8},{1,17},{9,25},{17,1},{25,9},{2,18},{10... | collective-permute-start | bytes 3145736 | tf_op jit(solution)/shard_map/ppermute | solution.py:151
  1251.4 5.5 collective-permute-start.12
  1255.0 5.2 collective-permute-start.13
  1260.4 5.0 collective-permute-start.14
  1263.5 5.7 collective-permute-start.15
  1270.1 5.3 collective-permute-start.16
  1273.5 5.2 collective-permute-start.17
  1278.8 5.9 collective-permute-start.18
  1282.8 5.7 collective-permute-start.19
Sparse Core Ops, SparseCore 0:
  312.5 37.6 all-reduce.18
  947.9 36.2 all-reduce.20
